TPU v7x, 256 devices: a whole 4x4x8 slice. The times are simulated.
256 devices in a mesh: gx: 8 (over y, x_lo), gy: 4 (over x_hi, core), gz: 8 (over z).
Axes of the slice: x: 4 (x_hi: 2, x_lo: 2; x = x_hi * 2 + x_lo), y: 4, z: 8, core: 2. Of those that a mesh axis runs over, the one named last changes fastest.
Arguments:
- tensor_blocks: bfloat16 [8, 4, 8, 3, 128, 128, 128], P('gx', 'gy', 'gz'), may hold values from 0 to 3
- fiber_mask: int32 [8, 4, 8, 3, 128, 128], P('gx', 'gy', 'gz'), may hold values 0 or 1
- block_coords: int32 [8, 4, 8, 3, 3], P('gx', 'gy', 'gz'), may hold values from 0 to 7, as said below
- block_counts: int32 [8, 4, 8], P('gx', 'gy', 'gz'), may hold values from 0 to 3, as said below
- factor_a: bfloat16 [8, 512, 256], P('gx', ('gy', 'gz')), may hold values from -0.59765625 to 0.59765625
- factor_b: bfloat16 [4, 1024, 256], P('gy', ('gx', 'gz')), may hold values from -0.59765625 to 0.59765625
- factor_c: bfloat16 [8, 512, 256], P('gz', ('gx', 'gy')), may hold values from -0.59765625 to 0.59765625
Outputs:
- grad_a: float32 [8, 512, 256], P('gx', ('gy', 'gz'))
- grad_b: float32 [4, 1024, 256], P('gy', ('gx', 'gz'))
- grad_c: float32 [8, 512, 256], P('gz', ('gx', 'gy'))
Inputs may be any that keep to these rules, and one draw needn't show every extreme that they name: `block_counts`: some sub-box holds exactly 3 blocks and some holds none, in every draw; slots at and past a sub-box's count hold no block. `block_coords`: the 3 columns of one sub-box name distinct blocks; row 0 is below 4, row 1 below 8, row 2 below 4.
All inputs are finite; a program needn't handle non-finite values. No bound on the sum of `fiber_mask` on one device may be relied on, other than what follows from the above.
Results may differ from a plain program's by a relative error of at most 0.0014.
Values may be sent and summed in bfloat16 or wider, within the bound.
A program may use at most 128 MiB of HBM per device.

v0:
```python
from functools import partial
import jax
import jax.numpy as jnp
from jax import lax
from jax.sharding import PartitionSpec as P

R = 256
BLK = 128
SLOTS = 3


def block_terms(rows_a, rows_b, rows_c, entries, fibers):
    khatri = (
        rows_b[:, None, :].astype(jnp.float32) * rows_c[None, :, :].astype(jnp.float32)
    ).astype(jnp.bfloat16)
    khatri = khatri.reshape(BLK * BLK, R)
    log_rate = jnp.einsum("ur,kr->uk", rows_a, khatri, preferred_element_type=jnp.float32)
    weight = fibers.astype(jnp.float32).reshape(BLK, BLK, 1)
    misfit = weight * (jnp.exp(log_rate.reshape(BLK, BLK, BLK)) - entries.astype(jnp.float32)) / BLK
    misfit = misfit.astype(jnp.bfloat16).reshape(BLK, BLK * BLK)
    part_a = jnp.dot(misfit, khatri, preferred_element_type=jnp.float32)
    folded = jnp.einsum("uk,ur->kr", misfit, rows_a, preferred_element_type=jnp.float32)
    folded = folded.astype(jnp.bfloat16).reshape(BLK, BLK, R)
    part_b = jnp.einsum("vwr,wr->vr", folded, rows_c, preferred_element_type=jnp.float32)
    part_c = jnp.einsum("vwr,vr->wr", folded, rows_b, preferred_element_type=jnp.float32)
    return (part_a, part_b, part_c)


def add_rows(total, start, part):
    current = lax.dynamic_slice_in_dim(total, start, BLK, 0)
    return lax.dynamic_update_slice_in_dim(total, current + part, start, 0)


def add_block(slot_index, coords, tensor_blocks, fiber_mask, slabs, totals):
    slab_rows_a, slab_rows_b, slab_rows_c = slabs
    grad_a, grad_b, grad_c = totals
    start_a = coords[0, slot_index] * BLK
    start_b = coords[1, slot_index] * BLK
    start_c = coords[2, slot_index] * BLK
    rows_a = lax.dynamic_slice_in_dim(slab_rows_a, start_a, BLK, 0)
    rows_b = lax.dynamic_slice_in_dim(slab_rows_b, start_b, BLK, 0)
    rows_c = lax.dynamic_slice_in_dim(slab_rows_c, start_c, BLK, 0)
    entries = tensor_blocks[0, 0, 0, slot_index]
    fibers = fiber_mask[0, 0, 0, slot_index]
    part_a, part_b, part_c = block_terms(rows_a, rows_b, rows_c, entries, fibers)
    return (
        add_rows(grad_a, start_a, part_a),
        add_rows(grad_b, start_b, part_b),
        add_rows(grad_c, start_c, part_c),
    )


def keep_totals(totals):
    return totals


def per_device(tensor_blocks, fiber_mask, block_coords, block_counts, factor_a, factor_b, factor_c):
    slab_rows_a = lax.all_gather(factor_a, ("gy", "gz"), axis=1, tiled=True)[0]
    slab_rows_b = lax.all_gather(factor_b, ("gx", "gz"), axis=1, tiled=True)[0]
    slab_rows_c = lax.all_gather(factor_c, ("gx", "gy"), axis=1, tiled=True)[0]
    slabs = (slab_rows_a, slab_rows_b, slab_rows_c)
    filled = block_counts[0, 0, 0]
    coords = block_coords[0, 0, 0]
    totals = (
        jnp.zeros(slab_rows_a.shape, jnp.float32),
        jnp.zeros(slab_rows_b.shape, jnp.float32),
        jnp.zeros(slab_rows_c.shape, jnp.float32),
    )
    for slot_index in range(SLOTS):
        adder = partial(add_block, slot_index, coords, tensor_blocks, fiber_mask, slabs)
        totals = lax.cond(slot_index < filled, adder, keep_totals, totals)
    terms_a, terms_b, terms_c = totals
    grad_a = lax.psum_scatter(terms_a[None], ("gy", "gz"), scatter_dimension=1, tiled=True)
    grad_b = lax.psum_scatter(terms_b[None], ("gx", "gz"), scatter_dimension=1, tiled=True)
    grad_c = lax.psum_scatter(terms_c[None], ("gx", "gy"), scatter_dimension=1, tiled=True)
    return (grad_a, grad_b, grad_c)


def solution(mesh):
    placed = (
        P("gx", "gy", "gz", None, None, None, None),
        P("gx", "gy", "gz", None, None, None),
        P("gx", "gy", "gz", None, None),
        P("gx", "gy", "gz"),
        P("gx", ("gy", "gz"), None),
        P("gy", ("gx", "gz"), None),
        P("gz", ("gx", "gy"), None),
    )
    return jax.shard_map(
        per_device,
        mesh=mesh,
        in_specs=placed,
        out_specs=(
            P("gx", ("gy", "gz"), None),
            P("gy", ("gx", "gz"), None),
            P("gz", ("gx", "gy"), None),
        ),
        check_vma=False,
    )
```

profile of v0, /device:TPU:4, one launch (start us, length us, event | category | flops | bytes accessed | tf_op | source)
XLA Modules:
  0.0 951.6 jit_solution(9491583259348897552)
XLA Ops:
  7.2 0.0 reduce-scatter.4.cloned.1.call-start
  7.2 161.8 %all_gather.10 = bf16[1,1024,256]{2,1,0:T(8,128)(2,1)S(1)} all-gather(bf16[1,16,256]{2,1,0:T(8,128)(2,1)} %param.18), channel_id=1, replica_groups=mesh['gx'=8,'gy'=4,'gz'=8] {'gx','gz'}, dimensions={1}, use_global_device_ids=true | all-gather | bytes 532480 | tf_op jit(solution)/shard_map/all_gather | solution.py:59
  169.0 65.1 %all_gather.9 = bf16[1,512,256]{2,1,0:T(8,128)(2,1)S(1)} all-gather(bf16[1,16,256]{2,1,0:T(8,128)(2,1)} %param.17), channel_id=1, replica_groups=mesh['gx'=8,'gy'=4,'gz'=8] {'gy','gz'}, dimensions={1}, use_global_device_ids=true | all-gather | bytes 270336 | tf_op jit(solution)/shard_map/all_gather | solution.py:58
  234.1 36.9 %all_gather.11 = bf16[1,512,256]{2,1,0:T(8,128)(2,1)S(1)} all-gather(bf16[1,16,256]{2,1,0:T(8,128)(2,1)} %param.19), channel_id=1, replica_groups=mesh['gx'=8,'gy'=4,'gz'=8] {'gx','gy'}, dimensions={1}, use_global_device_ids=true | all-gather | bytes 270336 | tf_op jit(solution)/shard_map/all_gather | solution.py:60
  271.0 0.7 copy.72
  272.4 36.4 %conditional.3 = (f32[512,256]{1,0:T(8,128)}, f32[1024,256]{1,0:T(8,128)}, f32[512,256]{1,0:T(8,128)}) conditional(s32[]{:T(128)} %bitcast.53, () %tuple.28, (s32[1,1,1,3,128,128]{5,4,3,2,1,0:T(8,128)}, s32[3,3]{1,0:T(4,128)S(1)}, bf16[512,256]{1,0:T(8,128)(2,1)S(1)}, bf16[1024,256]{1,0:T(8,128)(2,1)S(1)}, bf16[512,256]{1,0:T(8,128)(2,1)S(1)}, ...), branch_computations={%region_0.0_spmd, %region_1.0_spmd} | conditional | flops 3277930496 | bytes 64684284 | solution.py:71
  272.4 0.6 fusion.57
  274.9 0.0 copy-start
  274.9 17.6 %copy.14 = bf16[1,1,1,3,128,128,128]{4,6,5,3,2,1,0:T(8,128)(2,1)} copy(bf16[1,1,1,3,128,128,128]{6,5,4,3,2,1,0:T(8,128)(2,1)} %get-tuple-element.110) | data formatting | bytes 25165824 | tf_op jit(solution)/shard_map
  292.5 0.0 copy-done
  292.5 0.1 copy.13
  292.6 4.7 fusion.4
  297.3 2.6 multiply_reduce_fusion.1
  299.9 1.1 broadcast_in_dim.12
  301.0 0.7 bitcast_dynamic-update-slice_fusion.1
  301.7 2.8 multiply_reduce_fusion
  304.4 0.8 broadcast.26.clone.1
  305.3 0.7 bitcast_dynamic-update-slice_fusion
  305.9 0.8 broadcast.26.clone
  306.7 2.0 fusion.10
  308.8 34.9 %conditional.4 = ((f32[512,256]{1,0:T(8,128)}, f32[1024,256]{1,0:T(8,128)}, f32[512,256]{1,0:T(8,128)})) conditional(s32[]{:T(128)} %bitcast.52, (f32[512,256]{1,0:T(8,128)}, f32[1024,256]{1,0:T(8,128)}, f32[512,256]{1,0:T(8,128)}) %conditional.3, (s32[3,3]{1,0:T(4,128)S(1)}, f32[512,256]{1,0:T(8,128)}, s32[1,1,1,3,128,128]{5,4,3,2,1,0:T(8,128)}, ...), branch_computations={%region_2.0_spmd, %region_3.0_spmd} | conditional | flops 3278028800 | bytes 62980344 | solution.py:71
  308.8 0.6 fusion.58
  311.3 0.0 copy-start.1
  311.3 17.6 %copy.16 = bf16[1,1,1,3,128,128,128]{4,6,5,3,2,1,0:T(8,128)(2,1)} copy(bf16[1,1,1,3,128,128,128]{6,5,4,3,2,1,0:T(8,128)(2,1)} %get-tuple-element.117) | data formatting | bytes 25165824 | tf_op jit(solution)/shard_map
  328.8 0.0 copy-done.1
  328.8 0.1 copy.15
  329.0 4.7 fusion.21
  333.7 2.6 multiply_reduce_fusion.3
  336.3 2.8 multiply_reduce_fusion.2
  339.0 1.7 fusion.29
  340.7 2.9 fusion.28
  343.7 0.0 reduce-scatter.4.cloned.1.call-update
  343.7 0.0 reduce-scatter.8.cloned.1.call-start
  343.8 0.7 reduce-scatter.8.cloned.1.call-update
  344.5 0.0 reduce-scatter.6.cloned.1.call-start
  344.5 0.7 reduce-scatter.6.cloned.1.call-update
  345.2 142.6 %reduce-scatter.4.cloned.1.call-done = f32[1,16,256]{2,1,0:T(8,128)} async-done(((f32[1,512,256]{2,1,0:T(8,128)}), f32[1,16,256]{2,1,0:T(8,128)}) %reduce-scatter.4.cloned.1.call-update) | async-done | bytes 16400 | tf_op jit(solution)/shard_map/reduce_scatter | solution.py:73
  487.8 133.6 %reduce-scatter.8.cloned.1.call-done = f32[1,16,256]{2,1,0:T(8,128)} async-done(((f32[1,512,256]{2,1,0:T(8,128)}), f32[1,16,256]{2,1,0:T(8,128)}) %reduce-scatter.8.cloned.1.call-update) | async-done | bytes 16400 | tf_op jit(solution)/shard_map/reduce_scatter | solution.py:75
  621.4 323.7 %reduce-scatter.6.cloned.1.call-done = f32[1,16,256]{2,1,0:T(8,128)} async-done(((f32[1,1024,256]{2,1,0:T(8,128)}), f32[1,16,256]{2,1,0:T(8,128)}) %reduce-scatter.6.cloned.1.call-update) | async-done | bytes 16400 | tf_op jit(solution)/shard_map/reduce_scatter | solution.py:74
  (6 shorter events, 0.1 us)
Async XLA Ops:
  7.2 480.7 %reduce-scatter.4.cloned.1.call-start = ((), (), s32[]{:S(2)}) async-start(), calls=%async_computation.3 | async-start | bytes 540672 | tf_op jit(solution)/shard_map/reduce_scatter | solution.py:73
  274.9 17.6 %copy-start = (s32[1,1,1,3,128,128]{5,4,3,2,1,0:T(8,128)S(1)}, s32[1,1,1,3,128,128]{5,4,3,2,1,0:T(8,128)}, u32[]{:S(2)}) copy-start(s32[1,1,1,3,128,128]{5,4,3,2,1,0:T(8,128)} %get-tuple-element.105) | copy-start | bytes 589828 | tf_op jit(solution)/shard_map/cond
  311.3 17.6 %copy-start.1 = (s32[1,1,1,3,128,128]{5,4,3,2,1,0:T(8,128)S(1)}, s32[1,1,1,3,128,128]{5,4,3,2,1,0:T(8,128)}, u32[]{:S(2)}) copy-start(s32[1,1,1,3,128,128]{5,4,3,2,1,0:T(8,128)} %get-tuple-element.113) | copy-start | bytes 589828 | tf_op jit(solution)/shard_map/cond
  343.7 277.7 %reduce-scatter.8.cloned.1.call-start = ((), (), s32[]{:S(2)}) async-start(), calls=%async_computation.5 | async-start | bytes 540672 | tf_op jit(solution)/shard_map/reduce_scatter | solution.py:75
  344.5 600.7 %reduce-scatter.6.cloned.1.call-start = ((), (), s32[]{:S(2)}) async-start(), calls=%async_computation.4 | async-start | bytes 1064960 | tf_op jit(solution)/shard_map/reduce_scatter | solution.py:74
Sparse Core Ops, SparseCore 0:
  343.8 143.9 reduce-scatter.3
  490.9 130.5 reduce-scatter.7
  624.5 320.5 reduce-scatter.5
where the time goes:
time: 953 us; the launch traced here: 952 us
  waiting for transfers between devices  601 us (63%)
  blocking collectives  264 us (28%)
  local copies, waits for them, and re-layouts  41.3 us (4%)
  matrix products  19.5 us (2%)
  between operations  14.4 us (2%)
    reduce_scatter x1, waiting for transfers between devices, per_device(): lax.psum_scatter(terms_b[None], ('gx', 'gz'), scatter_dimension=1, tiled=...  324 us
    all_gather x1, blocking collectives, per_device(): slab_rows_b = lax.all_gather(factor_b, ('gx', 'gz'), axis=1, tiled=True)[0]  162 us
    reduce_scatter x1, waiting for transfers between devices, per_device(): lax.psum_scatter(terms_a[None], ('gy', 'gz'), scatter_dimension=1, tiled=...  143 us
    reduce_scatter x1, waiting for transfers between devices, per_device(): lax.psum_scatter(terms_c[None], ('gx', 'gy'), scatter_dimension=1, tiled=...  134 us
    all_gather x1, blocking collectives, per_device(): slab_rows_a = lax.all_gather(factor_a, ('gy', 'gz'), axis=1, tiled=True)[0]  65.1 us
    another operation x6, local copies, waits for them, and re-layouts  37 us
    all_gather x1, blocking collectives, per_device(): slab_rows_c = lax.all_gather(factor_c, ('gx', 'gy'), axis=1, tiled=True)[0]  36.9 us
  transfers between devices with their start and end apart: 3, of which 3 were waited for; matrix products, arithmetic and copies ran while one was open for 0% of the time, Pallas kernels for 0%

commit v1 on v0

--- a/solution.py
+++ b/solution.py
@@ -7,6 +7,19 @@
 R = 256
 BLK = 128
 SLOTS = 3
+
+
+def settle_domain(state):
+    v_next = jnp.concatenate(
+        lax.all_to_all(
+            jnp.stack([state] * lax.psum(1, axis_name=("gx", "gz")), axis=0),
+            axis_name=("gx", "gz"),
+            split_axis=0,
+            concat_axis=0,
+        ),
+        axis=1,
+    )
+    return v_next
 
 
 def block_terms(rows_a, rows_b, rows_c, entries, fibers):
@@ -56,7 +69,7 @@
 
 def per_device(tensor_blocks, fiber_mask, block_coords, block_counts, factor_a, factor_b, factor_c):
     slab_rows_a = lax.all_gather(factor_a, ("gy", "gz"), axis=1, tiled=True)[0]
-    slab_rows_b = lax.all_gather(factor_b, ("gx", "gz"), axis=1, tiled=True)[0]
+    slab_rows_b = settle_domain(factor_b)[0]
     slab_rows_c = lax.all_gather(factor_c, ("gx", "gy"), axis=1, tiled=True)[0]
     slabs = (slab_rows_a, slab_rows_b, slab_rows_c)
     filled = block_counts[0, 0, 0]

time: 953 us -> 813 us (0.85)
  blocking collectives: 264 us -> 110 us
  starting transfers between devices: 0.12 us -> 12.9 us
    all_gather x1 -> x0, blocking collectives: 162 us -> none  [per_device(): slab_rows_b = lax.all_gather(factor_b, ('gx', 'gz'), axis=1, tiled=True)[0]]
    all_to_all x0 -> x1, starting transfers between devices: none -> 12.7 us  [settle_domain(): lax.all_to_all(jnp.stack([state] * lax.psum(1, axis_name=('gx', 'gz')), a...]
    another operation x6 -> x7, local copies, waits for them, and re-layouts: 37 us -> 38.5 us
  transfers between devices with their start and end apart: 3 -> 4, of which waited for: 3 -> 3; matrix products, arithmetic and copies ran while one was open for 0% -> 0% of each run, Pallas kernels for 0% -> 0%
where the time goes in v1:
time: 813 us; the launch traced here: 812 us
  waiting for transfers between devices  601 us (74%)
  blocking collectives  110 us (14%)
  local copies, waits for them, and re-layouts  42.8 us (5%)
  matrix products  19.5 us (2%)
  between operations  14.4 us (2%)
  starting transfers between devices  12.9 us (2%)
    reduce_scatter x1, waiting for transfers between devices, per_device(): lax.psum_scatter(terms_b[None], ('gx', 'gz'), scatter_dimension=1, tiled=...  325 us
    reduce_scatter x1, waiting for transfers between devices, per_device(): lax.psum_scatter(terms_a[None], ('gy', 'gz'), scatter_dimension=1, tiled=...  141 us
    reduce_scatter x1, waiting for transfers between devices, per_device(): lax.psum_scatter(terms_c[None], ('gx', 'gy'), scatter_dimension=1, tiled=...  134 us
    all_gather x1, blocking collectives, per_device(): slab_rows_a = lax.all_gather(factor_a, ('gy', 'gz'), axis=1, tiled=True)[0]  71.7 us
    all_gather x1, blocking collectives, per_device(): slab_rows_c = lax.all_gather(factor_c, ('gx', 'gy'), axis=1, tiled=True)[0]  38.1 us
    another operation x6, local copies, waits for them, and re-layouts  36.9 us
  transfers between devices with their start and end apart: 4, of which 3 were waited for; matrix products, arithmetic and copies ran while one was open for 0% of the time, Pallas kernels for 0%

profile of v1, /device:TPU:4, one launch (start us, length us, event | category | flops | bytes accessed | tf_op | source)
XLA Modules:
  0.0 811.8 jit_solution(13700120536310571257)
XLA Ops:
  7.2 1.5 stack.2
  8.7 12.7 %all-to-all-start = ((bf16[64,1,16,256]{3,2,1,0:T(8,128)(2,1)}), bf16[64,1,16,256]{3,2,1,0:T(8,128)(2,1)S(1)}, u32[]{:S(2)}, u32[]{:S(2)}) async-start(bf16[64,1,16,256]{3,2,1,0:T(8,128)(2,1)} %stack.2), calls=%async_computation | async-start | bytes 1048576 | tf_op jit(solution)/shard_map/all_to_all | solution.py:14
  21.4 0.0 reduce-scatter.4.cloned.1.call-start
  21.5 0.7 copy.81
  22.8 71.7 %all_gather.6 = bf16[1,512,256]{2,1,0:T(8,128)(2,1)S(1)} all-gather(bf16[1,16,256]{2,1,0:T(8,128)(2,1)} %param.17), channel_id=1, replica_groups=mesh['gx'=8,'gy'=4,'gz'=8] {'gy','gz'}, dimensions={1}, use_global_device_ids=true | all-gather | bytes 270336 | tf_op jit(solution)/shard_map/all_gather | solution.py:71
  94.6 38.1 %all_gather.7 = bf16[1,512,256]{2,1,0:T(8,128)(2,1)S(1)} all-gather(bf16[1,16,256]{2,1,0:T(8,128)(2,1)} %param.19), channel_id=1, replica_groups=mesh['gx'=8,'gy'=4,'gz'=8] {'gx','gy'}, dimensions={1}, use_global_device_ids=true | all-gather | bytes 270336 | tf_op jit(solution)/shard_map/all_gather | solution.py:73
  132.7 0.0 all-to-all-done
  132.7 36.4 %conditional.3 = (f32[512,256]{1,0:T(8,128)}, f32[1024,256]{1,0:T(8,128)}, f32[512,256]{1,0:T(8,128)}) conditional(s32[]{:T(128)} %bitcast.53, () %tuple.28, (s32[1,1,1,3,128,128]{5,4,3,2,1,0:T(8,128)}, s32[3,3]{1,0:T(4,128)S(1)}, bf16[512,256]{1,0:T(8,128)(2,1)S(1)}, bf16[1024,256]{1,0:T(8,128)(2,1)S(1)}, bf16[512,256]{1,0:T(8,128)(2,1)S(1)}, ...), branch_computations={%region_0.0_spmd, %region_1.0_spmd} | conditional | flops 3277930496 | bytes 64684284 | solution.py:84
  132.7 0.6 fusion.57
  135.3 0.0 copy-start
  135.3 17.5 %copy.23 = bf16[1,1,1,3,128,128,128]{4,6,5,3,2,1,0:T(8,128)(2,1)} copy(bf16[1,1,1,3,128,128,128]{6,5,4,3,2,1,0:T(8,128)(2,1)} %get-tuple-element.134) | data formatting | bytes 25165824 | tf_op jit(solution)/shard_map
  152.8 0.0 copy-done
  152.8 0.1 copy.22
  153.0 4.7 fusion.4
  157.7 2.6 multiply_reduce_fusion.1
  160.3 1.1 broadcast_in_dim.12
  161.4 0.7 bitcast_dynamic-update-slice_fusion.1
  162.0 2.8 multiply_reduce_fusion
  164.8 0.8 broadcast.29.clone.1
  165.6 0.7 bitcast_dynamic-update-slice_fusion
  166.3 0.8 broadcast.29.clone
  167.1 2.0 fusion.10
  169.1 35.0 %conditional.4 = ((f32[512,256]{1,0:T(8,128)}, f32[1024,256]{1,0:T(8,128)}, f32[512,256]{1,0:T(8,128)})) conditional(s32[]{:T(128)} %bitcast.52, (f32[512,256]{1,0:T(8,128)}, f32[1024,256]{1,0:T(8,128)}, f32[512,256]{1,0:T(8,128)}) %conditional.3, (s32[3,3]{1,0:T(4,128)S(1)}, f32[512,256]{1,0:T(8,128)}, s32[1,1,1,3,128,128]{5,4,3,2,1,0:T(8,128)}, ...), branch_computations={%region_2.0_spmd, %region_3.0_spmd} | conditional | flops 3278028800 | bytes 62980344 | solution.py:84
  169.1 0.7 fusion.58
  171.8 0.0 copy-start.1
  171.8 17.5 %copy.25 = bf16[1,1,1,3,128,128,128]{4,6,5,3,2,1,0:T(8,128)(2,1)} copy(bf16[1,1,1,3,128,128,128]{6,5,4,3,2,1,0:T(8,128)(2,1)} %get-tuple-element.141) | data formatting | bytes 25165824 | tf_op jit(solution)/shard_map
  189.3 0.0 copy-done.1
  189.3 0.1 copy.24
  189.5 4.7 fusion.21
  194.1 2.6 multiply_reduce_fusion.3
  196.8 2.8 multiply_reduce_fusion.2
  199.5 1.7 fusion.29
  201.2 2.9 fusion.28
  204.2 0.0 reduce-scatter.4.cloned.1.call-update
  204.2 0.0 reduce-scatter.8.cloned.1.call-start
  204.3 0.7 reduce-scatter.8.cloned.1.call-update
  205.0 0.0 reduce-scatter.6.cloned.1.call-start
  205.0 0.7 reduce-scatter.6.cloned.1.call-update
  205.7 141.2 %reduce-scatter.4.cloned.1.call-done = f32[1,16,256]{2,1,0:T(8,128)} async-done(((f32[1,512,256]{2,1,0:T(8,128)}), f32[1,16,256]{2,1,0:T(8,128)}) %reduce-scatter.4.cloned.1.call-update) | async-done | bytes 16400 | tf_op jit(solution)/shard_map/reduce_scatter | solution.py:86
  346.9 133.6 %reduce-scatter.8.cloned.1.call-done = f32[1,16,256]{2,1,0:T(8,128)} async-done(((f32[1,512,256]{2,1,0:T(8,128)}), f32[1,16,256]{2,1,0:T(8,128)}) %reduce-scatter.8.cloned.1.call-update) | async-done | bytes 16400 | tf_op jit(solution)/shard_map/reduce_scatter | solution.py:88
  480.6 324.7 %reduce-scatter.6.cloned.1.call-done = f32[1,16,256]{2,1,0:T(8,128)} async-done(((f32[1,1024,256]{2,1,0:T(8,128)}), f32[1,16,256]{2,1,0:T(8,128)}) %reduce-scatter.6.cloned.1.call-update) | async-done | bytes 16400 | tf_op jit(solution)/shard_map/reduce_scatter | solution.py:87
  (6 shorter events, 0.1 us)
Async XLA Ops:
  8.7 124.0 %all-to-all-start = ((bf16[64,1,16,256]{3,2,1,0:T(8,128)(2,1)}), bf16[64,1,16,256]{3,2,1,0:T(8,128)(2,1)S(1)}, u32[]{:S(2)}, u32[]{:S(2)}) async-start(bf16[64,1,16,256]{3,2,1,0:T(8,128)(2,1)} %stack.2), calls=%async_computation | async-start | bytes 1048576 | tf_op jit(solution)/shard_map/all_to_all | solution.py:14
  21.4 325.5 %reduce-scatter.4.cloned.1.call-start = ((), (), s32[]{:S(2)}) async-start(), calls=%async_computation.4 | async-start | bytes 540672 | tf_op jit(solution)/shard_map/reduce_scatter | solution.py:86
  135.3 17.5 %copy-start = (s32[1,1,1,3,128,128]{5,4,3,2,1,0:T(8,128)S(1)}, s32[1,1,1,3,128,128]{5,4,3,2,1,0:T(8,128)}, u32[]{:S(2)}) copy-start(s32[1,1,1,3,128,128]{5,4,3,2,1,0:T(8,128)} %get-tuple-element.129) | copy-start | bytes 589828 | tf_op jit(solution)/shard_map/cond
  171.8 17.5 %copy-start.1 = (s32[1,1,1,3,128,128]{5,4,3,2,1,0:T(8,128)S(1)}, s32[1,1,1,3,128,128]{5,4,3,2,1,0:T(8,128)}, u32[]{:S(2)}) copy-start(s32[1,1,1,3,128,128]{5,4,3,2,1,0:T(8,128)} %get-tuple-element.137) | copy-start | bytes 589828 | tf_op jit(solution)/shard_map/cond
  204.2 276.4 %reduce-scatter.8.cloned.1.call-start = ((), (), s32[]{:S(2)}) async-start(), calls=%async_computation.6 | async-start | bytes 540672 | tf_op jit(solution)/shard_map/reduce_scatter | solution.py:88
  205.0 600.3 %reduce-scatter.6.cloned.1.call-start = ((), (), s32[]{:S(2)}) async-start(), calls=%async_computation.5 | async-start | bytes 1064960 | tf_op jit(solution)/shard_map/reduce_scatter | solution.py:87
Sparse Core Ops, SparseCore 0:
  204.3 142.5 reduce-scatter.3
  350.0 130.5 reduce-scatter.7
  483.6 321.6 reduce-scatter.5
